TPU v7x, 128 devices: a whole 4x4x4 slice. The times are simulated.
128 devices in a mesh: expert: 4 (over z), seq: 4 (over y), tensor: 8 (over x, core).
Axes of the slice: x: 4, y: 4, z: 4, core: 2. Of those that a mesh axis runs over, the one named last changes fastest.
Arguments:
- tokens: bfloat16 [3072, 7168], P(('expert', 'seq')), may hold values from -6 to 6
- grad_out: bfloat16 [3072, 7168], P(('expert', 'seq')), may hold values from -6 to 6
- expert_ids: int32 [3072, 2], P(('expert', 'seq')), may hold values from 0 to 3, all different within a row; in each aligned block of 192 rows (0 to 191, 192 to 383, ...) at most 128 rows name the same one
- route_weights: bfloat16 [3072, 2], P(('expert', 'seq')), may hold values from 0.099609375 to 1
- gate_weight: bfloat16 [4, 7168, 2048], P('expert', 'seq', 'tensor'), may hold values from -0.0625 to 0.0625
- up_weight: bfloat16 [4, 7168, 2048], P('expert', 'seq', 'tensor'), may hold values from -0.0625 to 0.0625
- down_weight: bfloat16 [4, 7168, 2048], P('expert', 'seq', 'tensor'), may hold values from -0.125 to 0.125
Outputs:
- grad_tokens: bfloat16 [3072, 7168], P(('expert', 'seq'), 'tensor')
- grad_route: float32 [3072, 2], P(('expert', 'seq'))
- grad_gate: float32 [4, 7168, 2048], P('expert', 'seq', 'tensor')
- grad_up: float32 [4, 7168, 2048], P('expert', 'seq', 'tensor')
- grad_down: float32 [4, 7168, 2048], P('expert', 'seq', 'tensor')
Inputs may be any that keep to these rules, and one draw needn't show every extreme that they name: `expert_ids`: the two ids of a row differ. Within each aligned block of 192 rows (the tokens of one group of the expert and seq axes) no expert is named by more than 128 rows, and in some block an expert is named by exactly 128 rows.
All inputs are finite; a program needn't handle non-finite values.
Results may differ from a plain program's by a relative error of at most 0.019.
Values may be sent and summed in bfloat16 or wider, within the bound.
A program may use at most 192 MiB of HBM per device.

v0:
```python
import jax
import jax.numpy as jnp
from jax import lax
from jax.sharding import PartitionSpec as P


def shards(tokens, grad_out, expert_ids, route_weights, gate_weight, up_weight, down_weight):
    expert_count = lax.axis_size("expert")
    seq_count = lax.axis_size("seq")
    tensor_count = lax.axis_size("tx") * lax.axis_size("core")
    core = lax.axis_index("core")
    local_count = gate_weight.shape[0]
    tok_rows = tokens.shape[0]
    model_width = tokens.shape[1]
    part_width = model_width // tensor_count
    per_peer = tok_rows // 6
    peer_count = expert_count * seq_count
    block_rows = local_count * per_peer
    slot_count = peer_count * block_rows
    flat_ids = expert_ids.reshape(-1)
    route_count = flat_ids.shape[0]
    onehot = (
        flat_ids[:, None] == jnp.arange(local_count * expert_count, dtype=jnp.int32)[None, :]
    ).astype(jnp.int32)
    before = jnp.cumsum(onehot, axis=0) - onehot
    ranking = jnp.sum(before * onehot, axis=1)
    local_expert = flat_ids % local_count
    dest_peer = flat_ids // local_count * seq_count + ranking % seq_count
    target = (dest_peer * local_count + local_expert) * per_peer + ranking // seq_count
    source = (
        jnp.full((slot_count,), -1, jnp.int32)
        .at[target]
        .set(jnp.arange(route_count, dtype=jnp.int32))
    )
    filled = source >= 0
    safe_source = jnp.maximum(source, 0)
    token_of = safe_source // 2
    keep = filled[:, None].astype(tokens.dtype)
    weight_send = (
        route_weights.reshape(-1)[safe_source] * filled.astype(route_weights.dtype)
    ).reshape(peer_count, block_rows)
    half = model_width // 2
    tokens_half = lax.dynamic_slice_in_dim(tokens, core * half, half, axis=1)
    grad_half = lax.dynamic_slice_in_dim(grad_out, core * half, half, axis=1)
    in_send = (tokens_half[token_of] * keep).reshape(peer_count, block_rows, half)
    out_send = (grad_half[token_of] * keep).reshape(peer_count, block_rows, half)
    in_mine, out_mine, weight_recv = (
        lax.all_to_all(in_send, ("expert", "seq"), split_axis=0, concat_axis=0, tiled=True),
        lax.all_to_all(out_send, ("expert", "seq"), split_axis=0, concat_axis=0, tiled=True),
        lax.all_to_all(weight_send, ("expert", "seq"), split_axis=0, concat_axis=0, tiled=True),
    )

    def join_halves(mine):
        other = lax.ppermute(mine, "core", [(0, 1), (1, 0)])
        first = jnp.where(core == 0, mine, other)
        second = jnp.where(core == 0, other, mine)
        return jnp.concatenate([first, second], axis=-1)

    in_recv = join_halves(in_mine)
    out_recv = join_halves(out_mine)

    def by_expert(values):
        shaped = values.reshape((peer_count, local_count, per_peer) + values.shape[2:])
        return jnp.swapaxes(shaped, 0, 1).reshape(
            (local_count, peer_count * per_peer) + values.shape[2:]
        )

    def by_peer(values):
        shaped = values.reshape((local_count, peer_count, per_peer) + values.shape[2:])
        return jnp.swapaxes(shaped, 0, 1).reshape((peer_count, block_rows) + values.shape[2:])

    in_rows = by_expert(in_recv)
    out_rows = by_expert(out_recv)
    prob = by_expert(weight_recv).astype(jnp.float32)[:, :, None]
    gate_full, up_full, down_full = (
        lax.all_gather(gate_weight, "seq", axis=1, tiled=True),
        lax.all_gather(up_weight, "seq", axis=1, tiled=True),
        lax.all_gather(down_weight, "seq", axis=1, tiled=True),
    )
    pre_gate = jnp.einsum("emd,edf->emf", in_rows, gate_full, preferred_element_type=jnp.float32)
    pre_up = jnp.einsum("emd,edf->emf", in_rows, up_full, preferred_element_type=jnp.float32)
    sigmoid_gate = jax.nn.sigmoid(pre_gate)
    silu_gate = pre_gate * sigmoid_gate
    hidden = silu_gate * pre_up
    hidden_low = hidden.astype(jnp.bfloat16)
    back_proj = jnp.einsum("emd,edf->emf", out_rows, down_full, preferred_element_type=jnp.float32)
    partial_scores = jnp.sum(hidden * back_proj, axis=2)
    scaled = (prob * out_rows.astype(jnp.float32)).astype(jnp.bfloat16)
    hidden_grad = prob * back_proj
    up_grad = (hidden_grad * silu_gate).astype(jnp.bfloat16)
    gate_grad = (
        hidden_grad * pre_up * sigmoid_gate * (1.0 + pre_gate * (1.0 - sigmoid_gate))
    ).astype(jnp.bfloat16)
    input_terms = jnp.einsum(
        "emf,edf->emd", gate_grad, gate_full, preferred_element_type=jnp.float32
    )
    input_terms = input_terms + jnp.einsum(
        "emf,edf->emd", up_grad, up_full, preferred_element_type=jnp.float32
    )
    route_scores = lax.psum(partial_scores, ("tx", "core"))
    input_shards = lax.psum_scatter(
        input_terms.astype(jnp.bfloat16), ("tx", "core"), scatter_dimension=2, tiled=True
    ).astype(jnp.float32)
    back_rows, back_scores = (
        lax.all_to_all(
            by_peer(input_shards).astype(jnp.bfloat16),
            ("expert", "seq"),
            split_axis=0,
            concat_axis=0,
            tiled=True,
        ).astype(jnp.float32),
        lax.all_to_all(
            by_peer(route_scores).astype(jnp.bfloat16),
            ("expert", "seq"),
            split_axis=0,
            concat_axis=0,
            tiled=True,
        ).astype(jnp.float32),
    )
    route_rows = back_rows.reshape(slot_count, part_width)[target].reshape(tok_rows, 2, part_width)
    grad_tokens = jnp.sum(route_rows, axis=1).astype(jnp.bfloat16)
    grad_route = back_scores.reshape(slot_count)[target].reshape(tok_rows, 2)
    gate_part = jnp.einsum("emd,emf->edf", in_rows, gate_grad, preferred_element_type=jnp.float32)
    up_part = jnp.einsum("emd,emf->edf", in_rows, up_grad, preferred_element_type=jnp.float32)
    down_part = jnp.einsum("emd,emf->edf", scaled, hidden_low, preferred_element_type=jnp.float32)
    grad_gate, grad_up, grad_down = (
        lax.psum_scatter(
            gate_part.astype(jnp.bfloat16), "seq", scatter_dimension=1, tiled=True
        ).astype(jnp.float32),
        lax.psum_scatter(
            up_part.astype(jnp.bfloat16), "seq", scatter_dimension=1, tiled=True
        ).astype(jnp.float32),
        lax.psum_scatter(
            down_part.astype(jnp.bfloat16), "seq", scatter_dimension=1, tiled=True
        ).astype(jnp.float32),
    )
    return (grad_tokens, grad_route, grad_gate, grad_up, grad_down)


def solution(mesh):
    shape = mesh.devices.shape
    mesh = jax.sharding.Mesh(
        mesh.devices.reshape(shape[0], shape[1], shape[2] // 2, 2), ("expert", "seq", "tx", "core")
    )
    tensor = ("tx", "core")
    placed = (
        P(("expert", "seq"), None),
        P(("expert", "seq"), None),
        P(("expert", "seq"), None),
        P(("expert", "seq"), None),
        P("expert", "seq", tensor),
        P("expert", "seq", tensor),
        P("expert", "seq", tensor),
    )
    return jax.shard_map(
        shards,
        mesh=mesh,
        in_specs=placed,
        out_specs=(
            P(("expert", "seq"), tensor),
            P(("expert", "seq"), None),
            P("expert", "seq", tensor),
            P("expert", "seq", tensor),
            P("expert", "seq", tensor),
        ),
        check_vma=False,
    )
```

profile of v0, /device:TPU:1, one launch (start us, length us, event | category | flops | bytes accessed | tf_op | source)
XLA Modules:
  0.0 511.5 jit_solution(3057996658511665825)
XLA Ops:
  29.6 6.8 %broadcast_multiply_fusion.1 = (bf16[16,32,3584]{2,1,0:T(8,128)(2,1)}, bf16[16,32,3584]{2,1,0:T(8,128)(2,1)}) fusion(bf16[16,32,3584]{2,1,0:T(8,128)(2,1)} %bitcast.74, bf16[16,32]{1,0:T(8,128)(2,1)S(1)} %reshape.301, bf16[16,32,3584]{2,1,0:T(8,128)(2,1)} %bitcast.73), kind=kLoop, calls=%fused_computation.34 | loop fusion | flops 3670016 | bytes 14681088 | tf_op jit(solution)/shard_map/mul | solution.py:46
  36.4 8.9 %all-to-all-start.2 = ((bf16[16,32,3584]{2,1,0:T(8,128)(2,1)}), bf16[16,32,3584]{2,1,0:T(8,128)(2,1)}, u32[]{:S(2)}, u32[]{:S(2)}) async-start(bf16[16,32,3584]{2,1,0:T(8,128)(2,1)} %get-tuple-element.30), calls=%async_computation.2 | async-start | bytes 7340032 | tf_op jit(solution)/shard_map/all_to_all | solution.py:48
  46.0 70.6 %all-to-all-done.2 = bf16[16,32,3584]{2,1,0:T(8,128)(2,1)} async-done(((bf16[16,32,3584]{2,1,0:T(8,128)(2,1)}), bf16[16,32,3584]{2,1,0:T(8,128)(2,1)}, u32[]{:S(2)}, u32[]{:S(2)}) %all-to-all-start.2) | async-done | bytes 3670048 | tf_op jit(solution)/shard_map/all_to_all | solution.py:48
  118.6 11.5 %all_to_all.31 = bf16[16,1,32]{2,1,0:T(2,128)(2,1)S(1)} all-to-all(bf16[16,1,32]{2,1,0:T(2,128)(2,1)S(1)} %all_to_all.25), channel_id=1, replica_groups=mesh['expert'=4,'seq'=4,'tx'=4,'core'=2] {'expert','seq'}, dimensions={0} | all-to-all | bytes 2048 | tf_op jit(solution)/shard_map/all_to_all | solution.py:50
  135.5 64.9 %all-to-all-done.1 = bf16[16,32,3584]{2,1,0:T(8,128)(2,1)} async-done(((bf16[16,32,3584]{2,1,0:T(8,128)(2,1)}), bf16[16,32,3584]{2,1,0:T(8,128)(2,1)}, u32[]{:S(2)}, u32[]{:S(2)}) %all-to-all-start.1) | async-done | bytes 3670048 | tf_op jit(solution)/shard_map/all_to_all | solution.py:49
  200.5 6.6 %collective-permute-start = (bf16[16,32,3584]{2,1,0:T(8,128)(2,1)}, bf16[16,32,3584]{2,1,0:T(8,128)(2,1)}, u32[]{:S(2)}, u32[]{:S(2)}) collective-permute-start(bf16[16,32,3584]{2,1,0:T(8,128)(2,1)} %all-to-all-done.1), channel_id=1, source_target_pairs={{0,1},{1,0},{2,3},{3,2},{4,5},{5,4},{6,7},{7,6},{8,9},{9,8},{10,11... | collective-permute-start | bytes 11010056 | tf_op jit(solution)/shard_map/ppermute | solution.py:54
  212.5 5.8 %pad_maximum_fusion.1 = bf16[16,32,7168]{2,1,0:T(8,128)(2,1)} fusion(bf16[16,32,3584]{2,1,0:T(8,128)(2,1)} %get-tuple-element.25, bf16[16,32,3584]{2,1,0:T(8,128)(2,1)S(1)} %get-tuple-element.24), kind=kLoop, calls=%fused_computation.16 | loop fusion | flops 14680064 | bytes 14680064 | tf_op jit(solution)/shard_map/concatenate | solution.py:57
  218.2 6.2 %fusion.7 = f32[512,256]{0,1:T(8,128)S(1)} fusion(bf16[512,7168]{1,0:T(8,128)(2,1)} %bitcast.67, bf16[1,7168,256]{2,1,0:T(8,128)(2,1)} %all-gather.8.cloned.1.call-done), kind=kOutput, calls=%fused_computation.21 | convolution fusion | flops 1879048192 | bytes 11534336 | tf_op jit(solution)/shard_map/emd,edf->emf/dot_general | solution.py:80
  224.5 6.2 %fusion.10 = f32[512,256]{0,1:T(8,128)S(1)} fusion(bf16[512,7168]{1,0:T(8,128)(2,1)} %bitcast.68, bf16[1,7168,256]{2,1,0:T(8,128)(2,1)} %all-gather.6.cloned.1.call-done), kind=kOutput, calls=%fused_computation.24 | convolution fusion | flops 1879048192 | bytes 11534336 | tf_op jit(solution)/shard_map/emd,edf->emf/dot_general | solution.py:81
  230.7 5.6 %broadcast_select_fusion.3 = (bf16[16,32,3584]{2,1,0:T(8,128)(2,1)S(1)}, bf16[16,32,3584]{2,1,0:T(8,128)(2,1)}) fusion(bf16[16,32,3584]{2,1,0:T(8,128)(2,1)} %all-to-all-done.1, bf16[16,32,3584]{2,1,0:T(8,128)(2,1)} %collective-permute-done, pred[]{:T(512)S(6)} %eq.42), kind=kLoop, calls=%fused_computation.31 | loop fusion | flops 3670016 | bytes 14680065 | tf_op jit(solution)/shard_map/jit(_where)/select_n | solution.py:55
  236.3 5.8 %pad_maximum_fusion = bf16[16,32,7168]{2,1,0:T(8,128)(2,1)} fusion(bf16[16,32,3584]{2,1,0:T(8,128)(2,1)} %get-tuple-element.23, bf16[16,32,3584]{2,1,0:T(8,128)(2,1)S(1)} %get-tuple-element.22), kind=kLoop, calls=%fused_computation.15 | loop fusion | flops 14680064 | bytes 14680064 | tf_op jit(solution)/shard_map/concatenate | solution.py:57
  242.1 6.6 %multiply_reduce_fusion = (f32[512]{0:T(512)S(1)}, bf16[512,256]{0,1:T(8,128)(2,1)S(1)}, bf16[512,256]{0,1:T(8,128)(2,1)S(1)}) fusion(f32[512,256]{0,1:T(8,128)S(1)} %fusion.10, f32[512,256]{0,1:T(8,128)S(1)} %fusion.7, f32[512]{0:T(512)S(1)} %reshape.300, bf16[512,7168]{1,0:T(8,128)(2,1)} %bitcast.75, bf16[1,7168,256]{2,1,0:T(8,128)(2,1)} %all-gather.4.cloned.1.call-done), kind=kOutput, calls=%fused_computation.36 | convolution fusion | flops 1881275904 | bytes 12587008 | tf_op jit(solution)/shard_map/emd,edf->emf/dot_general | solution.py:86
  248.7 7.3 %fusion.5 = f32[512,7168]{1,0:T(8,128)} fusion(bf16[512,256]{0,1:T(8,128)(2,1)S(1)} %get-tuple-element.27, bf16[1,7168,256]{2,1,0:T(8,128)(2,1)S(1)} %copy-done.1), kind=kOutput, calls=%fused_computation.19 | convolution fusion | flops 1879048192 | bytes 18612224 | tf_op jit(solution)/shard_map/emf,edf->emd/dot_general | solution.py:94
  256.0 10.6 %fusion = bf16[1,512,7168]{2,1,0:T(8,128)(2,1)} fusion(f32[512,7168]{1,0:T(8,128)} %fusion.5, bf16[512,256]{0,1:T(8,128)(2,1)S(1)} %get-tuple-element.28, bf16[1,7168,256]{2,1,0:T(8,128)(2,1)S(1)} %copy-done), kind=kOutput, calls=%fused_computation.8 | convolution fusion | flops 1886388224 | bytes 25952256 | tf_op jit(solution)/shard_map/emf,edf->emd/dot_general | solution.py:97
  266.6 31.4 %copy.30 = bf16[1,512,7168]{1,0,2:T(2,128)(2,1)} copy(bf16[1,512,7168]{2,1,0:T(8,128)(2,1)} %fusion) | data formatting | bytes 14680064
  298.1 10.3 %copy.36 = bf16[7168,1,512]{2,0,1:T(8,128)(2,1)} copy(bf16[7168,1,512]{2,1,0:T(2,128)(2,1)} %bitcast.71) | data formatting | bytes 14680064
  308.5 8.0 %fusion.3 = bf16[1,7168,256]{2,1,0:T(8,128)(2,1)} fusion(bf16[512,7168]{1,0:T(8,128)(2,1)} %bitcast.76, f32[512]{0:T(512)S(1)} %reshape.300, f32[512,256]{0,1:T(8,128)S(1)} %fusion.10, f32[512,256]{0,1:T(8,128)S(1)} %fusion.7), kind=kOutput, calls=%fused_computation.14 | convolution fusion | flops 1892679680 | bytes 12060672 | tf_op jit(solution)/shard_map/emd,emf->edf/dot_general | solution.py:125
  316.6 7.1 %fusion.1 = bf16[1,7168,256]{2,1,0:T(8,128)(2,1)} fusion(bf16[512,7168]{1,0:T(8,128)(2,1)} %bitcast.69, bf16[512,256]{0,1:T(8,128)(2,1)S(1)} %get-tuple-element.27), kind=kOutput, calls=%fused_computation.12 | convolution fusion | flops 1880883200 | bytes 11272192 | tf_op jit(solution)/shard_map/emd,emf->edf/dot_general | solution.py:123
  323.8 7.2 %fusion.2 = bf16[1,7168,256]{2,1,0:T(8,128)(2,1)} fusion(bf16[512,7168]{1,0:T(8,128)(2,1)} %bitcast.70, bf16[512,256]{0,1:T(8,128)(2,1)S(1)} %get-tuple-element.28), kind=kOutput, calls=%fused_computation.13 | convolution fusion | flops 1880883200 | bytes 11272192 | tf_op jit(solution)/shard_map/emd,emf->edf/dot_general | solution.py:124
  330.9 23.5 %psum.7 = bf16[1,512]{1,0:T(2,128)(2,1)S(1)} all-reduce(f32[1,512]{1,0:T(1,128)S(1)} %bitcast.78), channel_id=1, replica_groups=mesh['expert'=4,'seq'=4,'tx'=4,'core'=2] {'tx','core'}, use_global_device_ids=true, to_apply=%region_7.8 | all-reduce | flops 512 | bytes 3072 | tf_op jit(solution)/shard_map/psum | solution.py:100
  365.1 6.0 %all-to-all-start.3 = ((bf16[16,32,896]{2,1,0:T(8,128)(2,1)}), bf16[16,32,896]{2,1,0:T(8,128)(2,1)S(1)}, u32[]{:S(2)}, u32[]{:S(2)}) async-start(bf16[16,32,896]{2,1,0:T(8,128)(2,1)} %bitcast.9), calls=%async_computation.3 | async-start | bytes 1835008 | tf_op jit(solution)/shard_map/all_to_all | solution.py:105
  374.8 32.5 %reduce-scatter.11.cloned.1.call-done = bf16[1,1792,256]{2,1,0:T(8,128)(2,1)} async-done(((bf16[1,7168,256]{2,1,0:T(8,128)(2,1)}), bf16[1,1792,256]{2,1,0:T(8,128)(2,1)}) %reduce-scatter.11.cloned.1.call-update) | async-done | bytes 917520 | tf_op jit(solution)/shard_map/reduce_scatter | solution.py:133
  409.9 41.9 %reduce-scatter.7.cloned.1.call-done = bf16[1,1792,256]{2,1,0:T(8,128)(2,1)} async-done(((bf16[1,7168,256]{2,1,0:T(8,128)(2,1)}), bf16[1,1792,256]{2,1,0:T(8,128)(2,1)}) %reduce-scatter.7.cloned.1.call-update) | async-done | bytes 917520 | tf_op jit(solution)/shard_map/reduce_scatter | solution.py:127
  454.3 42.1 %reduce-scatter.9.cloned.1.call-done = bf16[1,1792,256]{2,1,0:T(8,128)(2,1)} async-done(((bf16[1,7168,256]{2,1,0:T(8,128)(2,1)}), bf16[1,1792,256]{2,1,0:T(8,128)(2,1)}) %reduce-scatter.9.cloned.1.call-update) | async-done | bytes 917520 | tf_op jit(solution)/shard_map/reduce_scatter | solution.py:130
  (76 shorter events, 63.4 us)
Async XLA Ops:
  7.2 211.1 %all-gather.8.cloned.1.call-start = ((), (), s32[]{:S(2)}) async-start(), calls=%async_computation.11 | async-start | bytes 4587520 | tf_op jit(solution)/shard_map/all_gather | solution.py:76
  36.4 80.3 %all-to-all-start.2 = ((bf16[16,32,3584]{2,1,0:T(8,128)(2,1)}), bf16[16,32,3584]{2,1,0:T(8,128)(2,1)}, u32[]{:S(2)}, u32[]{:S(2)}) async-start(bf16[16,32,3584]{2,1,0:T(8,128)(2,1)} %get-tuple-element.30), calls=%async_computation.2 | async-start | bytes 7340032 | tf_op jit(solution)/shard_map/all_to_all | solution.py:48
  45.3 179.2 %all-gather.6.cloned.1.call-start = ((), (), s32[]{:S(2)}) async-start(), calls=%async_computation.10 | async-start | bytes 4587520 | tf_op jit(solution)/shard_map/all_gather | solution.py:77
  116.7 90.4 %collective-permute-start.1 = (bf16[16,32,3584]{2,1,0:T(8,128)(2,1)}, bf16[16,32,3584]{2,1,0:T(8,128)(2,1)}, u32[]{:S(2)}, u32[]{:S(2)}) collective-permute-start(bf16[16,32,3584]{2,1,0:T(8,128)(2,1)} %all-to-all-done.2), channel_id=1, source_target_pairs={{0,1},{1,0},{2,3},{3,2},{4,5},{5,4},{6,7},{7,6},{8,9},{9,8},{10,11... | collective-permute-start | bytes 11010056 | tf_op jit(solution)/shard_map/ppermute | solution.py:54
  130.1 70.3 %all-to-all-start.1 = ((bf16[16,32,3584]{2,1,0:T(8,128)(2,1)}), bf16[16,32,3584]{2,1,0:T(8,128)(2,1)}, u32[]{:S(2)}, u32[]{:S(2)}) async-start(bf16[16,32,3584]{2,1,0:T(8,128)(2,1)} %get-tuple-element.29), calls=%async_computation.1 | async-start | bytes 7340032 | tf_op jit(solution)/shard_map/all_to_all | solution.py:49
  134.6 107.4 %all-gather.4.cloned.1.call-start = ((), (), s32[]{:S(2)}) async-start(), calls=%async_computation.9 | async-start | bytes 4587520 | tf_op jit(solution)/shard_map/all_gather | solution.py:78
  135.4 223.5 %reduce-scatter.13.cloned.1.call-start = ((), (), s32[]{:S(2)}) async-start(), calls=%async_computation.15 | async-start | bytes 8257536
  200.5 30.3 %collective-permute-start = (bf16[16,32,3584]{2,1,0:T(8,128)(2,1)}, bf16[16,32,3584]{2,1,0:T(8,128)(2,1)}, u32[]{:S(2)}, u32[]{:S(2)}) collective-permute-start(bf16[16,32,3584]{2,1,0:T(8,128)(2,1)} %all-to-all-done.1), channel_id=1, source_target_pairs={{0,1},{1,0},{2,3},{3,2},{4,5},{5,4},{6,7},{7,6},{8,9},{9,8},{10,11... | collective-permute-start | bytes 11010056 | tf_op jit(solution)/shard_map/ppermute | solution.py:54
  242.1 6.6 %copy-start.1 = (bf16[1,7168,256]{2,1,0:T(8,128)(2,1)S(1)}, bf16[1,7168,256]{2,1,0:T(8,128)(2,1)}, u32[]{:S(2)}) copy-start(bf16[1,7168,256]{2,1,0:T(8,128)(2,1)} %all-gather.8.cloned.1.call-done) | copy-start | bytes 11010052
  248.7 7.4 %copy-start = (bf16[1,7168,256]{2,1,0:T(8,128)(2,1)S(1)}, bf16[1,7168,256]{2,1,0:T(8,128)(2,1)}, u32[]{:S(2)}) copy-start(bf16[1,7168,256]{2,1,0:T(8,128)(2,1)} %all-gather.6.cloned.1.call-done) | copy-start | bytes 11010052
  308.4 98.9 %reduce-scatter.11.cloned.1.call-start = ((), (), s32[]{:S(2)}) async-start(), calls=%async_computation.14 | async-start | bytes 4587520 | tf_op jit(solution)/shard_map/reduce_scatter | solution.py:133
  316.5 135.2 %reduce-scatter.7.cloned.1.call-start = ((), (), s32[]{:S(2)}) async-start(), calls=%async_computation.12 | async-start | bytes 4587520 | tf_op jit(solution)/shard_map/reduce_scatter | solution.py:127
  323.7 172.7 %reduce-scatter.9.cloned.1.call-start = ((), (), s32[]{:S(2)}) async-start(), calls=%async_computation.13 | async-start | bytes 4587520 | tf_op jit(solution)/shard_map/reduce_scatter | solution.py:130
  355.1 9.9 %all-to-all-start.4 = ((bf16[16,1,32]{2,1,0:T(2,128)(2,1)}), bf16[16,1,32]{2,1,0:T(2,128)(2,1)S(1)}, u32[]{:S(2)}, u32[]{:S(2)}) async-start(bf16[16,1,32]{2,1,0:T(2,128)(2,1)} %convert_element_type.144), calls=%async_computation.4 | async-start | bytes 16384 | tf_op jit(solution)/shard_map/all_to_all | solution.py:112
  365.1 133.9 %all-to-all-start.3 = ((bf16[16,32,896]{2,1,0:T(8,128)(2,1)}), bf16[16,32,896]{2,1,0:T(8,128)(2,1)S(1)}, u32[]{:S(2)}, u32[]{:S(2)}) async-start(bf16[16,32,896]{2,1,0:T(8,128)(2,1)} %bitcast.9), calls=%async_computation.3 | async-start | bytes 1835008 | tf_op jit(solution)/shard_map/all_to_all | solution.py:105
Sparse Core Ops, SparseCore 0:
  9.7 68.7 all-gather.7
  80.2 55.4 all-gather.5
  137.3 70.2 all-gather.3
  308.6 43.6 reduce-scatter.12
  354.5 52.7 reduce-scatter.10
  409.6 42.1 reduce-scatter.6
  454.2 42.2 reduce-scatter.8
where the time goes:
time: 519 us; the launch traced here: 512 us
  waiting for transfers between devices  255 us (49%)
  local copies, waits for them, and re-layouts  73.9 us (14%)
  matrix products  59.3 us (11%)
  other arithmetic  42 us (8%)
  blocking collectives  35 us (7%)
  starting transfers between devices  31.7 us (6%)
  between operations  14.6 us (3%)
    all_to_all x1, waiting for transfers between devices, shards(): lax.all_to_all(in_send, ('expert', 'seq'), split_axis=0, concat_axis=0, t...  70.6 us
    all_to_all x1, waiting for transfers between devices, shards(): lax.all_to_all(out_send, ('expert', 'seq'), split_axis=0, concat_axis=0,...  64.9 us
    unnamed x11, local copies, waits for them, and re-layouts  49.6 us
    reduce_scatter x1, waiting for transfers between devices, shards(): lax.psum_scatter(up_part.astype(jnp.bfloat16), 'seq', scatter_dimension=1...  42.1 us
    reduce_scatter x1, waiting for transfers between devices, shards(): lax.psum_scatter(gate_part.astype(jnp.bfloat16), 'seq', scatter_dimension...  41.9 us
    reduce_scatter x1, waiting for transfers between devices, shards(): lax.psum_scatter(down_part.astype(jnp.bfloat16), 'seq', scatter_dimension...  32.5 us
    psum x1, blocking collectives, shards(): route_scores = lax.psum(partial_scores, ('tx', 'core'))  23.5 us
    all_to_all x1, blocking collectives, shards(): lax.all_to_all(weight_send, ('expert', 'seq'), split_axis=0, concat_axis=...  11.5 us
  transfers between devices with their start and end apart: 13, of which 6 were waited for; matrix products, arithmetic and copies ran while one was open for 20% of the time, Pallas kernels for 0%

commit v1 on v0

--- a/solution.py
+++ b/solution.py
@@ -2,6 +2,11 @@
 import jax.numpy as jnp
 from jax import lax
 from jax.sharding import PartitionSpec as P
+
+
+def resolve_the_shifts_all(block_here):
+    f_now = lax.psum(lax.psum(block_here, "core"), "tx")
+    return f_now
 
 
 def shards(tokens, grad_out, expert_ids, route_weights, gate_weight, up_weight, down_weight):
@@ -97,7 +102,7 @@
     input_terms = input_terms + jnp.einsum(
         "emf,edf->emd", up_grad, up_full, preferred_element_type=jnp.float32
     )
-    route_scores = lax.psum(partial_scores, ("tx", "core"))
+    route_scores = resolve_the_shifts_all(partial_scores)
     input_shards = lax.psum_scatter(
         input_terms.astype(jnp.bfloat16), ("tx", "core"), scatter_dimension=2, tiled=True
     ).astype(jnp.float32)

time: 519 us -> 519 us (level)
  blocking collectives: 35 us -> 28.7 us
  waiting for transfers between devices: 255 us -> 261 us
    psum x1 -> x2, blocking collectives: 23.5 us -> 17.1 us  [resolve_the_shifts_all(): f_now = lax.psum(lax.psum(block_here, 'core'), 'tx')]
    reduce_scatter x1, waiting for transfers between devices: 32.5 us -> 38.7 us  [shards(): lax.psum_scatter(down_part.astype(jnp.bfloat16), 'seq', scatter_dimension...]
where the time goes in v1:
time: 519 us; the launch traced here: 511 us
  waiting for transfers between devices  261 us (50%)
  local copies, waits for them, and re-layouts  73.9 us (14%)
  matrix products  59.3 us (11%)
  other arithmetic  42 us (8%)
  starting transfers between devices  31.7 us (6%)
  blocking collectives  28.7 us (6%)
  between operations  14.6 us (3%)
    all_to_all x1, waiting for transfers between devices, shards(): lax.all_to_all(in_send, ('expert', 'seq'), split_axis=0, concat_axis=0, t...  70.6 us
    all_to_all x1, waiting for transfers between devices, shards(): lax.all_to_all(out_send, ('expert', 'seq'), split_axis=0, concat_axis=0,...  64.9 us
    unnamed x11, local copies, waits for them, and re-layouts  49.6 us
    reduce_scatter x1, waiting for transfers between devices, shards(): lax.psum_scatter(up_part.astype(jnp.bfloat16), 'seq', scatter_dimension=1...  42.1 us
    reduce_scatter x1, waiting for transfers between devices, shards(): lax.psum_scatter(gate_part.astype(jnp.bfloat16), 'seq', scatter_dimension...  42 us
    reduce_scatter x1, waiting for transfers between devices, shards(): lax.psum_scatter(down_part.astype(jnp.bfloat16), 'seq', scatter_dimension...  38.7 us
    psum x2, blocking collectives, resolve_the_shifts_all(): f_now = lax.psum(lax.psum(block_here, 'core'), 'tx')  17.1 us
    all_to_all x1, blocking collectives, shards(): lax.all_to_all(weight_send, ('expert', 'seq'), split_axis=0, concat_axis=...  11.5 us
  transfers between devices with their start and end apart: 13, of which 6 were waited for; matrix products, arithmetic and copies ran while one was open for 20% of the time, Pallas kernels for 0%

profile of v1, /device:TPU:1, one launch (start us, length us, event | category | flops | bytes accessed | tf_op | source)
XLA Modules:
  0.0 511.4 jit_solution(2117565139440539300)
XLA Ops:
  29.6 6.8 %broadcast_multiply_fusion.1 = (bf16[16,32,3584]{2,1,0:T(8,128)(2,1)}, bf16[16,32,3584]{2,1,0:T(8,128)(2,1)}) fusion(bf16[16,32,3584]{2,1,0:T(8,128)(2,1)} %bitcast.74, bf16[16,32]{1,0:T(8,128)(2,1)S(1)} %reshape.301, bf16[16,32,3584]{2,1,0:T(8,128)(2,1)} %bitcast.73), kind=kLoop, calls=%fused_computation.34 | loop fusion | flops 3670016 | bytes 14681088 | tf_op jit(solution)/shard_map/mul | solution.py:51
  36.4 8.9 %all-to-all-start.2 = ((bf16[16,32,3584]{2,1,0:T(8,128)(2,1)}), bf16[16,32,3584]{2,1,0:T(8,128)(2,1)}, u32[]{:S(2)}, u32[]{:S(2)}) async-start(bf16[16,32,3584]{2,1,0:T(8,128)(2,1)} %get-tuple-element.30), calls=%async_computation.2 | async-start | bytes 7340032 | tf_op jit(solution)/shard_map/all_to_all | solution.py:53
  46.0 70.6 %all-to-all-done.2 = bf16[16,32,3584]{2,1,0:T(8,128)(2,1)} async-done(((bf16[16,32,3584]{2,1,0:T(8,128)(2,1)}), bf16[16,32,3584]{2,1,0:T(8,128)(2,1)}, u32[]{:S(2)}, u32[]{:S(2)}) %all-to-all-start.2) | async-done | bytes 3670048 | tf_op jit(solution)/shard_map/all_to_all | solution.py:53
  118.6 11.5 %all_to_all.31 = bf16[16,1,32]{2,1,0:T(2,128)(2,1)S(1)} all-to-all(bf16[16,1,32]{2,1,0:T(2,128)(2,1)S(1)} %all_to_all.25), channel_id=1, replica_groups=mesh['expert'=4,'seq'=4,'tx'=4,'core'=2] {'expert','seq'}, dimensions={0} | all-to-all | bytes 2048 | tf_op jit(solution)/shard_map/all_to_all | solution.py:55
  135.5 64.9 %all-to-all-done.1 = bf16[16,32,3584]{2,1,0:T(8,128)(2,1)} async-done(((bf16[16,32,3584]{2,1,0:T(8,128)(2,1)}), bf16[16,32,3584]{2,1,0:T(8,128)(2,1)}, u32[]{:S(2)}, u32[]{:S(2)}) %all-to-all-start.1) | async-done | bytes 3670048 | tf_op jit(solution)/shard_map/all_to_all | solution.py:54
  200.5 6.6 %collective-permute-start = (bf16[16,32,3584]{2,1,0:T(8,128)(2,1)}, bf16[16,32,3584]{2,1,0:T(8,128)(2,1)}, u32[]{:S(2)}, u32[]{:S(2)}) collective-permute-start(bf16[16,32,3584]{2,1,0:T(8,128)(2,1)} %all-to-all-done.1), channel_id=1, source_target_pairs={{0,1},{1,0},{2,3},{3,2},{4,5},{5,4},{6,7},{7,6},{8,9},{9,8},{10,11... | collective-permute-start | bytes 11010056 | tf_op jit(solution)/shard_map/ppermute | solution.py:59
  212.5 5.8 %pad_maximum_fusion.1 = bf16[16,32,7168]{2,1,0:T(8,128)(2,1)} fusion(bf16[16,32,3584]{2,1,0:T(8,128)(2,1)} %get-tuple-element.25, bf16[16,32,3584]{2,1,0:T(8,128)(2,1)S(1)} %get-tuple-element.24), kind=kLoop, calls=%fused_computation.16 | loop fusion | flops 14680064 | bytes 14680064 | tf_op jit(solution)/shard_map/concatenate | solution.py:62
  218.2 6.2 %fusion.7 = f32[512,256]{0,1:T(8,128)S(1)} fusion(bf16[512,7168]{1,0:T(8,128)(2,1)} %bitcast.67, bf16[1,7168,256]{2,1,0:T(8,128)(2,1)} %all-gather.8.cloned.1.call-done), kind=kOutput, calls=%fused_computation.21 | convolution fusion | flops 1879048192 | bytes 11534336 | tf_op jit(solution)/shard_map/emd,edf->emf/dot_general | solution.py:85
  224.5 6.2 %fusion.10 = f32[512,256]{0,1:T(8,128)S(1)} fusion(bf16[512,7168]{1,0:T(8,128)(2,1)} %bitcast.68, bf16[1,7168,256]{2,1,0:T(8,128)(2,1)} %all-gather.6.cloned.1.call-done), kind=kOutput, calls=%fused_computation.24 | convolution fusion | flops 1879048192 | bytes 11534336 | tf_op jit(solution)/shard_map/emd,edf->emf/dot_general | solution.py:86
  230.7 5.6 %broadcast_select_fusion.3 = (bf16[16,32,3584]{2,1,0:T(8,128)(2,1)S(1)}, bf16[16,32,3584]{2,1,0:T(8,128)(2,1)}) fusion(bf16[16,32,3584]{2,1,0:T(8,128)(2,1)} %all-to-all-done.1, bf16[16,32,3584]{2,1,0:T(8,128)(2,1)} %collective-permute-done, pred[]{:T(512)S(6)} %eq.42), kind=kLoop, calls=%fused_computation.31 | loop fusion | flops 3670016 | bytes 14680065 | tf_op jit(solution)/shard_map/jit(_where)/select_n | solution.py:60
  236.3 5.8 %pad_maximum_fusion = bf16[16,32,7168]{2,1,0:T(8,128)(2,1)} fusion(bf16[16,32,3584]{2,1,0:T(8,128)(2,1)} %get-tuple-element.23, bf16[16,32,3584]{2,1,0:T(8,128)(2,1)S(1)} %get-tuple-element.22), kind=kLoop, calls=%fused_computation.15 | loop fusion | flops 14680064 | bytes 14680064 | tf_op jit(solution)/shard_map/concatenate | solution.py:62
  242.1 6.6 %multiply_reduce_fusion = (f32[512]{0:T(512)S(1)}, bf16[512,256]{0,1:T(8,128)(2,1)S(1)}, bf16[512,256]{0,1:T(8,128)(2,1)S(1)}) fusion(f32[512,256]{0,1:T(8,128)S(1)} %fusion.10, f32[512,256]{0,1:T(8,128)S(1)} %fusion.7, f32[512]{0:T(512)S(1)} %reshape.300, bf16[512,7168]{1,0:T(8,128)(2,1)} %bitcast.75, bf16[1,7168,256]{2,1,0:T(8,128)(2,1)} %all-gather.4.cloned.1.call-done), kind=kOutput, calls=%fused_computation.36 | convolution fusion | flops 1881275904 | bytes 12587008 | tf_op jit(solution)/shard_map/emd,edf->emf/dot_general | solution.py:91
  248.7 7.3 %fusion.5 = f32[512,7168]{1,0:T(8,128)} fusion(bf16[512,256]{0,1:T(8,128)(2,1)S(1)} %get-tuple-element.27, bf16[1,7168,256]{2,1,0:T(8,128)(2,1)S(1)} %copy-done.1), kind=kOutput, calls=%fused_computation.19 | convolution fusion | flops 1879048192 | bytes 18612224 | tf_op jit(solution)/shard_map/emf,edf->emd/dot_general | solution.py:99
  256.0 10.6 %fusion = bf16[1,512,7168]{2,1,0:T(8,128)(2,1)} fusion(f32[512,7168]{1,0:T(8,128)} %fusion.5, bf16[512,256]{0,1:T(8,128)(2,1)S(1)} %get-tuple-element.28, bf16[1,7168,256]{2,1,0:T(8,128)(2,1)S(1)} %copy-done), kind=kOutput, calls=%fused_computation.8 | convolution fusion | flops 1886388224 | bytes 25952256 | tf_op jit(solution)/shard_map/emf,edf->emd/dot_general | solution.py:102
  266.6 31.4 %copy.30 = bf16[1,512,7168]{1,0,2:T(2,128)(2,1)} copy(bf16[1,512,7168]{2,1,0:T(8,128)(2,1)} %fusion) | data formatting | bytes 14680064
  298.1 10.3 %copy.36 = bf16[7168,1,512]{2,0,1:T(8,128)(2,1)} copy(bf16[7168,1,512]{2,1,0:T(2,128)(2,1)} %bitcast.71) | data formatting | bytes 14680064
  308.5 8.0 %fusion.3 = bf16[1,7168,256]{2,1,0:T(8,128)(2,1)} fusion(bf16[512,7168]{1,0:T(8,128)(2,1)} %bitcast.76, f32[512]{0:T(512)S(1)} %reshape.300, f32[512,256]{0,1:T(8,128)S(1)} %fusion.10, f32[512,256]{0,1:T(8,128)S(1)} %fusion.7), kind=kOutput, calls=%fused_computation.14 | convolution fusion | flops 1892679680 | bytes 12060672 | tf_op jit(solution)/shard_map/emd,emf->edf/dot_general | solution.py:130
  316.6 7.1 %fusion.1 = bf16[1,7168,256]{2,1,0:T(8,128)(2,1)} fusion(bf16[512,7168]{1,0:T(8,128)(2,1)} %bitcast.69, bf16[512,256]{0,1:T(8,128)(2,1)S(1)} %get-tuple-element.27), kind=kOutput, calls=%fused_computation.12 | convolution fusion | flops 1880883200 | bytes 11272192 | tf_op jit(solution)/shard_map/emd,emf->edf/dot_general | solution.py:128
  323.8 7.2 %fusion.2 = bf16[1,7168,256]{2,1,0:T(8,128)(2,1)} fusion(bf16[512,7168]{1,0:T(8,128)(2,1)} %bitcast.70, bf16[512,256]{0,1:T(8,128)(2,1)S(1)} %get-tuple-element.28), kind=kOutput, calls=%fused_computation.13 | convolution fusion | flops 1880883200 | bytes 11272192 | tf_op jit(solution)/shard_map/emd,emf->edf/dot_general | solution.py:129
  333.4 14.7 %psum.15 = bf16[1,512]{1,0:T(2,128)(2,1)S(1)} all-reduce(f32[1,512]{1,0:T(1,128)S(1)} %psum.14), channel_id=1, replica_groups=mesh['expert'=4,'seq'=4,'tx'=4,'core'=2] {'tx'}, use_global_device_ids=true, to_apply=%region_8.9 | all-reduce | flops 512 | bytes 3072 | tf_op jit(solution)/shard_map/psum | solution.py:8
  358.7 6.0 %all-to-all-start.3 = ((bf16[16,32,896]{2,1,0:T(8,128)(2,1)}), bf16[16,32,896]{2,1,0:T(8,128)(2,1)S(1)}, u32[]{:S(2)}, u32[]{:S(2)}) async-start(bf16[16,32,896]{2,1,0:T(8,128)(2,1)} %bitcast.9), calls=%async_computation.3 | async-start | bytes 1835008 | tf_op jit(solution)/shard_map/all_to_all | solution.py:110
  368.5 38.7 %reduce-scatter.11.cloned.1.call-done = bf16[1,1792,256]{2,1,0:T(8,128)(2,1)} async-done(((bf16[1,7168,256]{2,1,0:T(8,128)(2,1)}), bf16[1,1792,256]{2,1,0:T(8,128)(2,1)}) %reduce-scatter.11.cloned.1.call-update) | async-done | bytes 917520 | tf_op jit(solution)/shard_map/reduce_scatter | solution.py:138
  409.7 42.0 %reduce-scatter.7.cloned.1.call-done = bf16[1,1792,256]{2,1,0:T(8,128)(2,1)} async-done(((bf16[1,7168,256]{2,1,0:T(8,128)(2,1)}), bf16[1,1792,256]{2,1,0:T(8,128)(2,1)}) %reduce-scatter.7.cloned.1.call-update) | async-done | bytes 917520 | tf_op jit(solution)/shard_map/reduce_scatter | solution.py:132
  454.2 42.1 %reduce-scatter.9.cloned.1.call-done = bf16[1,1792,256]{2,1,0:T(8,128)(2,1)} async-done(((bf16[1,7168,256]{2,1,0:T(8,128)(2,1)}), bf16[1,1792,256]{2,1,0:T(8,128)(2,1)}) %reduce-scatter.9.cloned.1.call-update) | async-done | bytes 917520 | tf_op jit(solution)/shard_map/reduce_scatter | solution.py:135
  (77 shorter events, 65.8 us)
Async XLA Ops:
  7.2 211.1 %all-gather.8.cloned.1.call-start = ((), (), s32[]{:S(2)}) async-start(), calls=%async_computation.11 | async-start | bytes 4587520 | tf_op jit(solution)/shard_map/all_gather | solution.py:81
  36.4 80.3 %all-to-all-start.2 = ((bf16[16,32,3584]{2,1,0:T(8,128)(2,1)}), bf16[16,32,3584]{2,1,0:T(8,128)(2,1)}, u32[]{:S(2)}, u32[]{:S(2)}) async-start(bf16[16,32,3584]{2,1,0:T(8,128)(2,1)} %get-tuple-element.30), calls=%async_computation.2 | async-start | bytes 7340032 | tf_op jit(solution)/shard_map/all_to_all | solution.py:53
  45.3 179.2 %all-gather.6.cloned.1.call-start = ((), (), s32[]{:S(2)}) async-start(), calls=%async_computation.10 | async-start | bytes 4587520 | tf_op jit(solution)/shard_map/all_gather | solution.py:82
  116.7 90.4 %collective-permute-start.1 = (bf16[16,32,3584]{2,1,0:T(8,128)(2,1)}, bf16[16,32,3584]{2,1,0:T(8,128)(2,1)}, u32[]{:S(2)}, u32[]{:S(2)}) collective-permute-start(bf16[16,32,3584]{2,1,0:T(8,128)(2,1)} %all-to-all-done.2), channel_id=1, source_target_pairs={{0,1},{1,0},{2,3},{3,2},{4,5},{5,4},{6,7},{7,6},{8,9},{9,8},{10,11... | collective-permute-start | bytes 11010056 | tf_op jit(solution)/shard_map/ppermute | solution.py:59
  130.1 70.3 %all-to-all-start.1 = ((bf16[16,32,3584]{2,1,0:T(8,128)(2,1)}), bf16[16,32,3584]{2,1,0:T(8,128)(2,1)}, u32[]{:S(2)}, u32[]{:S(2)}) async-start(bf16[16,32,3584]{2,1,0:T(8,128)(2,1)} %get-tuple-element.29), calls=%async_computation.1 | async-start | bytes 7340032 | tf_op jit(solution)/shard_map/all_to_all | solution.py:54
  134.6 107.4 %all-gather.4.cloned.1.call-start = ((), (), s32[]{:S(2)}) async-start(), calls=%async_computation.9 | async-start | bytes 4587520 | tf_op jit(solution)/shard_map/all_gather | solution.py:83
  135.4 217.1 %reduce-scatter.13.cloned.1.call-start = ((), (), s32[]{:S(2)}) async-start(), calls=%async_computation.15 | async-start | bytes 8257536
  200.5 30.3 %collective-permute-start = (bf16[16,32,3584]{2,1,0:T(8,128)(2,1)}, bf16[16,32,3584]{2,1,0:T(8,128)(2,1)}, u32[]{:S(2)}, u32[]{:S(2)}) collective-permute-start(bf16[16,32,3584]{2,1,0:T(8,128)(2,1)} %all-to-all-done.1), channel_id=1, source_target_pairs={{0,1},{1,0},{2,3},{3,2},{4,5},{5,4},{6,7},{7,6},{8,9},{9,8},{10,11... | collective-permute-start | bytes 11010056 | tf_op jit(solution)/shard_map/ppermute | solution.py:59
  242.1 6.6 %copy-start.1 = (bf16[1,7168,256]{2,1,0:T(8,128)(2,1)S(1)}, bf16[1,7168,256]{2,1,0:T(8,128)(2,1)}, u32[]{:S(2)}) copy-start(bf16[1,7168,256]{2,1,0:T(8,128)(2,1)} %all-gather.8.cloned.1.call-done) | copy-start | bytes 11010052
  248.7 7.4 %copy-start = (bf16[1,7168,256]{2,1,0:T(8,128)(2,1)S(1)}, bf16[1,7168,256]{2,1,0:T(8,128)(2,1)}, u32[]{:S(2)}) copy-start(bf16[1,7168,256]{2,1,0:T(8,128)(2,1)} %all-gather.6.cloned.1.call-done) | copy-start | bytes 11010052
  308.4 98.7 %reduce-scatter.11.cloned.1.call-start = ((), (), s32[]{:S(2)}) async-start(), calls=%async_computation.14 | async-start | bytes 4587520 | tf_op jit(solution)/shard_map/reduce_scatter | solution.py:138
  316.5 135.2 %reduce-scatter.7.cloned.1.call-start = ((), (), s32[]{:S(2)}) async-start(), calls=%async_computation.12 | async-start | bytes 4587520 | tf_op jit(solution)/shard_map/reduce_scatter | solution.py:132
  323.7 172.6 %reduce-scatter.9.cloned.1.call-start = ((), (), s32[]{:S(2)}) async-start(), calls=%async_computation.13 | async-start | bytes 4587520 | tf_op jit(solution)/shard_map/reduce_scatter | solution.py:135
  348.8 9.9 %all-to-all-start.4 = ((bf16[16,1,32]{2,1,0:T(2,128)(2,1)}), bf16[16,1,32]{2,1,0:T(2,128)(2,1)S(1)}, u32[]{:S(2)}, u32[]{:S(2)}) async-start(bf16[16,1,32]{2,1,0:T(2,128)(2,1)} %convert_element_type.144), calls=%async_computation.4 | async-start | bytes 16384 | tf_op jit(solution)/shard_map/all_to_all | solution.py:117
  358.7 140.2 %all-to-all-start.3 = ((bf16[16,32,896]{2,1,0:T(8,128)(2,1)}), bf16[16,32,896]{2,1,0:T(8,128)(2,1)S(1)}, u32[]{:S(2)}, u32[]{:S(2)}) async-start(bf16[16,32,896]{2,1,0:T(8,128)(2,1)} %bitcast.9), calls=%async_computation.3 | async-start | bytes 1835008 | tf_op jit(solution)/shard_map/all_to_all | solution.py:110
Sparse Core Ops, SparseCore 0:
  9.7 68.7 all-gather.7
  80.2 55.4 all-gather.5
  137.3 70.2 all-gather.3
  308.6 43.6 reduce-scatter.12
  354.5 52.5 reduce-scatter.10
  409.4 42.2 reduce-scatter.6
  454.1 42.2 reduce-scatter.8
